TPU v7x, 256 devices: a whole 4x4x8 slice. The times are simulated.
256 devices in a mesh: blk: 16 (over z, x_lo), mode: 16 (over y, x_hi, core).
Axes of the slice: x: 4 (x_hi: 2, x_lo: 2; x = x_hi * 2 + x_lo), y: 4, z: 8, core: 2. Of those that a mesh axis runs over, the one named last changes fastest.
Arguments:
- chaos_field: float32 [448, 65536], P('mode', 'blk'), may hold values from -6 to 6
- kl_field: float32 [13, 65536], P(None, 'blk'), may hold values from -1.6 to 4, as said below
- partner: int32 [12, 2, 448], P(None, None, 'mode'), may hold values from 0 to 447, each once within a row
- chaos_coef: float32 [12, 2, 448], P(None, None, 'mode'), may hold values from 0.5 to 2
- cell_count: int32 [16], P('blk'), may hold values from 2048 to 4096, as said below
- face_count: int32 [16, 4], P('blk'), may hold values from 0 to 128, as said below
- face_cells: int32 [16, 4, 128], P('blk'), may hold values from 0 to 4095, as said below
Outputs:
- applied: float32 [448, 65536], P('mode', 'blk')
Inputs may be any that keep to these rules, and one draw needn't show every extreme that they name: A block's live cells are its first cell_count cells, a whole number of rows of 128; some block is full. `face_count`: slots are the neighbouring blocks at offsets -2, -1, +1, +2 of the block index; a pair of blocks has the same count seen from either side, and 0 where the neighbour does not exist. `face_cells`: entry f of a slot pairs with entry f of the neighbour's opposite slot; entries below the count name live cells. `kl_field`: row 0 lies in 0.5 to 4.
All inputs are finite; a program needn't handle non-finite values.
Results may differ from a plain program's by a relative error of at most 0.000068.
Values sent between devices are 32-bit elements; how exact they have to be, the bound alone decides.
No kernel may reach another device: no remote copies, remote signals or barrier semaphores. Data moves between devices by JAX's collectives and lax.ppermute only.
A program may use at most 64 MiB of HBM per device.

v0:
```python
import jax
import jax.numpy as jnp
from jax import lax
from jax.sharding import PartitionSpec as P

GZ = 128
SLOT_OFFSETS = (-2, -1, 1, 2)
HIGHEST = lax.Precision.HIGHEST


def shifted(value, axis, steps):
    count = lax.axis_size(axis)
    first, last = (max(0, -steps), min(count, count - steps))
    return lax.ppermute(value, axis, [(source, source + steps) for source in range(first, last)])


def grid_terms(values, conduct, alive_grid):
    down_coef = (
        0.5
        * (conduct[..., 1:, :] + conduct[..., :-1, :])
        * (alive_grid[..., 1:, :] * alive_grid[..., :-1, :])
    )
    down_step = down_coef * (values[..., :-1, :] - values[..., 1:, :])
    side_coef = (
        0.5
        * (conduct[..., :, 1:] + conduct[..., :, :-1])
        * (alive_grid[..., :, 1:] * alive_grid[..., :, :-1])
    )
    side_step = side_coef * (values[..., :, :-1] - values[..., :, 1:])
    leading = [(0, 0)] * (values.ndim - 2)
    result = jnp.pad(down_step, leading + [(0, 1), (0, 0)]) - jnp.pad(
        down_step, leading + [(1, 0), (0, 0)]
    )
    return (
        result
        + jnp.pad(side_step, leading + [(0, 0), (0, 1)])
        - jnp.pad(side_step, leading + [(0, 0), (1, 0)])
    )


def operator_terms(values, conduct, alive_grid, own_flat, face_coef, cells_here):
    modes_here = values.shape[0]
    inside = values[:, :cells_here]
    grid_values = inside.reshape(modes_here, alive_grid.shape[0], alive_grid.shape[1])
    grid_part = grid_terms(grid_values, conduct.reshape(alive_grid.shape), alive_grid).reshape(
        modes_here, cells_here
    )
    own_values = jnp.take(inside, own_flat, axis=1)
    face_part = face_coef[None, :] * (own_values - values[:, cells_here:])
    return (grid_part, face_part)


def neighbour_faces(outgoing):
    pieces = []
    for slot_index, offset in enumerate(SLOT_OFFSETS):
        pieces.append(shifted(outgoing[:, 3 - slot_index], "blk", -offset))
    return jnp.stack(pieces, axis=1)


def per_device(chaos_field, kl_field, partner, chaos_coef, cell_count, face_count, face_cells):
    modes_here, cells_here = chaos_field.shape
    rows_grid = cells_here // GZ
    alive_flag = (lax.iota(jnp.int32, cells_here) < cell_count[0]).astype(jnp.float32)
    alive_grid = alive_flag.reshape(rows_grid, GZ)
    masked = chaos_field * alive_flag[None, :]
    face_limit = face_cells.shape[2]
    own_flat = face_cells[0].reshape(-1)
    face_alive = (
        (lax.iota(jnp.int32, face_limit)[None, :] < face_count[0][:, None])
        .astype(jnp.float32)
        .reshape(-1)
    )
    own_conduct = jnp.take(kl_field, own_flat, axis=1)
    outgoing = jnp.concatenate([jnp.take(masked, own_flat, axis=1), own_conduct], axis=0)
    outgoing = outgoing.reshape(outgoing.shape[0], 4, face_limit)
    arrived = neighbour_faces(outgoing)
    arrived = arrived.reshape(arrived.shape[0], 4 * face_limit)
    remote_field = arrived[:modes_here]
    remote_conduct = arrived[modes_here:]
    face_coefs = 0.5 * (own_conduct + remote_conduct) * face_alive[None, :]
    extended = jnp.concatenate([masked, remote_field], axis=1)
    all_modes = modes_here * lax.axis_size("mode")
    mode_ids = lax.iota(jnp.int32, all_modes)
    mixing_rows = jnp.sum(
        jnp.where(partner[:, :, :, None] == mode_ids, chaos_coef[:, :, :, None], 0.0), axis=1
    )
    random_terms = mixing_rows.shape[0]
    grid_zero, face_zero = operator_terms(
        extended, kl_field[0], alive_grid, own_flat, face_coefs[0], cells_here
    )
    own_term = grid_zero.at[:, own_flat].add(face_zero)
    starting = (
        jnp.zeros((modes_here, cells_here), jnp.float32),
        jnp.zeros((modes_here, 4 * face_limit), jnp.float32),
    )
    portion = lax.all_gather(extended, "mode", axis=0, tiled=True)

    def one_term(kl_index, partial_value):
        mixed_part = jnp.dot(
            mixing_rows[kl_index], portion, precision=HIGHEST, preferred_element_type=jnp.float32
        )
        grid_part, face_part = operator_terms(
            mixed_part,
            kl_field[kl_index + 1],
            alive_grid,
            own_flat,
            face_coefs[kl_index + 1],
            cells_here,
        )
        return (partial_value[0] + grid_part, partial_value[1] + face_part)

    grid_sum, face_sum = lax.fori_loop(0, random_terms, one_term, starting)
    summed = grid_sum.at[:, own_flat].add(face_sum) + own_term
    return summed * alive_flag[None, :]


def solution(mesh):
    in_specs = (
        P("mode", "blk"),
        P(None, "blk"),
        P(None, None, "mode"),
        P(None, None, "mode"),
        P("blk"),
        P("blk", None),
        P("blk", None, None),
    )
    out_specs = P("mode", "blk")
    return jax.shard_map(
        per_device, mesh=mesh, in_specs=in_specs, out_specs=out_specs, check_vma=False
    )
```

profile of v0, /device:TPU:1, one launch (start us, length us, event | category | flops | bytes accessed | tf_op | source)
XLA Modules:
  0.0 323.9 jit_solution(10393485028300684983)
XLA Ops:
  15.9 4.4 %collective-permute-start = (f32[41,128]{1,0:T(8,128)S(1)}, f32[41,128]{1,0:T(8,128)S(1)}, u32[]{:S(2)}, u32[]{:S(2)}) collective-permute-start(f32[41,128]{1,0:T(8,128)S(1)} %bitcast.99), channel_id=1, source_target_pairs={{0,32},{16,48},{32,64},{48,80},{64,96},{80,112},{96,128},{112,144}... | collective-permute-start | bytes 62984 | tf_op jit(solution)/shard_map/ppermute | solution.py:14
  20.3 3.1 collective-permute-start.1
  26.1 2.1 collective-permute-done.2
  28.2 3.1 collective-permute-done.3
  35.0 2.0 copy.81
  37.1 3.0 fusion.12
  42.3 78.4 %all-gather.3.cloned.1.call-done = f32[16,28,4608]{2,1,0:T(8,128)} async-done(((f32[1,28,4608]{2,1,0:T(8,128)}), f32[16,28,4608]{2,1,0:T(8,128)}) %all-gather.3.cloned.1.call-update) | async-done | bytes 8257552 | tf_op jit(solution)/shard_map/all_gather | solution.py:96
  120.7 9.2 %reshape.167 = f32[448,4608]{1,0:T(8,128)} reshape(f32[16,28,4608]{2,1,0:T(8,128)} %all-gather.3.cloned.1.call-done) | data formatting | bytes 16515072
  129.9 171.5 %while.18 = (s32[]{:T(128)}, f32[28,4096]{1,0:T(8,128)}, f32[28,512]{1,0:T(8,128)S(1)}, f32[13,4096]{1,0:T(8,128)S(1)}, f32[31,128]{1,0:T(8,128)}, /*index=5*/f3...) while((s32[]{:T(128)}, f32[28,4096]{1,0:T(8,128)}, ...), condition=%wide.region_2.4_spmd.clone, body=%wide.region_1.3_spmd.clone.sunk | while | flops 694757632 | bytes 20811360 | solution.py:112
  130.8 7.1 %fusion.31 = f32[28,4608]{1,0:T(8,128)S(1)} fusion(f32[448,4608]{1,0:T(8,128)} %get-tuple-element.445, f32[12,28,448]{2,1,0:T(8,128)} %get-tuple-element.444, s32[]{:T(128)} %get-tuple-element.424), kind=kOutput, calls=%fused_computation.13.clone.1 | convolution fusion | flops 693633024 | bytes 8839680 | tf_op jit(solution)/shard_map/while/body/eval_jaxpr/dot_general | solution.py:99
  144.1 7.1 %fusion.31 = f32[28,4608]{1,0:T(8,128)S(1)} fusion(f32[448,4608]{1,0:T(8,128)} %get-tuple-element.445, f32[12,28,448]{2,1,0:T(8,128)} %get-tuple-element.444, s32[]{:T(128)} %get-tuple-element.424), kind=kOutput, calls=%fused_computation.13.clone.1 | convolution fusion | flops 693633024 | bytes 8839680 | tf_op jit(solution)/shard_map/while/body/eval_jaxpr/dot_general | solution.py:99
  158.5 7.1 %fusion.31 = f32[28,4608]{1,0:T(8,128)S(1)} fusion(f32[448,4608]{1,0:T(8,128)} %get-tuple-element.445, f32[12,28,448]{2,1,0:T(8,128)} %get-tuple-element.444, s32[]{:T(128)} %get-tuple-element.424), kind=kOutput, calls=%fused_computation.13.clone.1 | convolution fusion | flops 693633024 | bytes 8839680 | tf_op jit(solution)/shard_map/while/body/eval_jaxpr/dot_general | solution.py:99
  172.9 7.1 %fusion.31 = f32[28,4608]{1,0:T(8,128)S(1)} fusion(f32[448,4608]{1,0:T(8,128)} %get-tuple-element.445, f32[12,28,448]{2,1,0:T(8,128)} %get-tuple-element.444, s32[]{:T(128)} %get-tuple-element.424), kind=kOutput, calls=%fused_computation.13.clone.1 | convolution fusion | flops 693633024 | bytes 8839680 | tf_op jit(solution)/shard_map/while/body/eval_jaxpr/dot_general | solution.py:99
  187.3 7.1 %fusion.31 = f32[28,4608]{1,0:T(8,128)S(1)} fusion(f32[448,4608]{1,0:T(8,128)} %get-tuple-element.445, f32[12,28,448]{2,1,0:T(8,128)} %get-tuple-element.444, s32[]{:T(128)} %get-tuple-element.424), kind=kOutput, calls=%fused_computation.13.clone.1 | convolution fusion | flops 693633024 | bytes 8839680 | tf_op jit(solution)/shard_map/while/body/eval_jaxpr/dot_general | solution.py:99
  201.7 7.1 %fusion.31 = f32[28,4608]{1,0:T(8,128)S(1)} fusion(f32[448,4608]{1,0:T(8,128)} %get-tuple-element.445, f32[12,28,448]{2,1,0:T(8,128)} %get-tuple-element.444, s32[]{:T(128)} %get-tuple-element.424), kind=kOutput, calls=%fused_computation.13.clone.1 | convolution fusion | flops 693633024 | bytes 8839680 | tf_op jit(solution)/shard_map/while/body/eval_jaxpr/dot_general | solution.py:99
  216.0 7.1 %fusion.31 = f32[28,4608]{1,0:T(8,128)S(1)} fusion(f32[448,4608]{1,0:T(8,128)} %get-tuple-element.445, f32[12,28,448]{2,1,0:T(8,128)} %get-tuple-element.444, s32[]{:T(128)} %get-tuple-element.424), kind=kOutput, calls=%fused_computation.13.clone.1 | convolution fusion | flops 693633024 | bytes 8839680 | tf_op jit(solution)/shard_map/while/body/eval_jaxpr/dot_general | solution.py:99
  230.4 7.1 %fusion.31 = f32[28,4608]{1,0:T(8,128)S(1)} fusion(f32[448,4608]{1,0:T(8,128)} %get-tuple-element.445, f32[12,28,448]{2,1,0:T(8,128)} %get-tuple-element.444, s32[]{:T(128)} %get-tuple-element.424), kind=kOutput, calls=%fused_computation.13.clone.1 | convolution fusion | flops 693633024 | bytes 8839680 | tf_op jit(solution)/shard_map/while/body/eval_jaxpr/dot_general | solution.py:99
  244.8 7.1 %fusion.31 = f32[28,4608]{1,0:T(8,128)S(1)} fusion(f32[448,4608]{1,0:T(8,128)} %get-tuple-element.445, f32[12,28,448]{2,1,0:T(8,128)} %get-tuple-element.444, s32[]{:T(128)} %get-tuple-element.424), kind=kOutput, calls=%fused_computation.13.clone.1 | convolution fusion | flops 693633024 | bytes 8839680 | tf_op jit(solution)/shard_map/while/body/eval_jaxpr/dot_general | solution.py:99
  259.2 7.1 %fusion.31 = f32[28,4608]{1,0:T(8,128)S(1)} fusion(f32[448,4608]{1,0:T(8,128)} %get-tuple-element.445, f32[12,28,448]{2,1,0:T(8,128)} %get-tuple-element.444, s32[]{:T(128)} %get-tuple-element.424), kind=kOutput, calls=%fused_computation.13.clone.1 | convolution fusion | flops 693633024 | bytes 8839680 | tf_op jit(solution)/shard_map/while/body/eval_jaxpr/dot_general | solution.py:99
  273.6 7.1 %fusion.31 = f32[28,4608]{1,0:T(8,128)S(1)} fusion(f32[448,4608]{1,0:T(8,128)} %get-tuple-element.445, f32[12,28,448]{2,1,0:T(8,128)} %get-tuple-element.444, s32[]{:T(128)} %get-tuple-element.424), kind=kOutput, calls=%fused_computation.13.clone.1 | convolution fusion | flops 693633024 | bytes 8839680 | tf_op jit(solution)/shard_map/while/body/eval_jaxpr/dot_general | solution.py:99
  288.0 7.1 %fusion.31 = f32[28,4608]{1,0:T(8,128)S(1)} fusion(f32[448,4608]{1,0:T(8,128)} %get-tuple-element.445, f32[12,28,448]{2,1,0:T(8,128)} %get-tuple-element.444, s32[]{:T(128)} %get-tuple-element.424), kind=kOutput, calls=%fused_computation.13.clone.1 | convolution fusion | flops 693633024 | bytes 8839680 | tf_op jit(solution)/shard_map/while/body/eval_jaxpr/dot_general | solution.py:99
  302.5 3.0 copy.82
  305.6 2.4 bitcast_add_fusion
  308.0 7.6 %scatter_fusion = f32[28,4096]{0,1:T(8,128)S(1)} fusion(f32[28,4096]{0,1:T(8,128)S(1)} %bitcast_add_fusion, s32[1024]{0:T(1024)S(1)} %bitcast.104, f32[1024,28]{1,0:T(8,128)S(1)} %copy.84), kind=kCustom, calls=%fused_computation.3 | custom fusion | flops 28672 | bytes 348160 | tf_op jit(solution)/shard_map/add | solution.py:113
  (341 shorter events, 103.9 us)
Async XLA Ops:
  6.5 114.1 %all-gather.3.cloned.1.call-start = ((), (), s32[]{:S(2)}) async-start(), calls=%async_computation | async-start | bytes 10027008 | tf_op jit(solution)/shard_map/all_gather | solution.py:96
  7.9 6.7 %copy-start.7 = (pred[512]{0:T(512)(128)(4,1)}, pred[512]{0:T(512)(128)(4,1)S(1)}, u32[]{:S(2)}) copy-start(pred[512]{0:T(512)(128)(4,1)S(1)} %compare_and_fusion.1) | copy-start | bytes 1540
  8.6 0.6 copy-start.3
  10.3 2.6 copy-start.1
  10.3 2.6 copy-start
  12.9 1.9 copy-start.5
  14.8 17.8 %copy-start.9 = (s32[12,2,28]{2,1,0:T(2,128)S(1)}, s32[12,2,28]{2,1,0:T(2,128)}, u32[]{:S(2)}) copy-start(s32[12,2,28]{2,1,0:T(2,128)} %param.13) | copy-start | bytes 8068
  14.8 18.0 %copy-start.10 = (f32[12,2,28]{2,1,0:T(2,128)S(1)}, f32[12,2,28]{2,1,0:T(2,128)}, u32[]{:S(2)}) copy-start(f32[12,2,28]{2,1,0:T(2,128)} %param.14) | copy-start | bytes 8068
  15.9 10.1 %collective-permute-start = (f32[41,128]{1,0:T(8,128)S(1)}, f32[41,128]{1,0:T(8,128)S(1)}, u32[]{:S(2)}, u32[]{:S(2)}) collective-permute-start(f32[41,128]{1,0:T(8,128)S(1)} %bitcast.99), channel_id=1, source_target_pairs={{0,32},{16,48},{32,64},{48,80},{64,96},{80,112},{96,128},{112,144}... | collective-permute-start | bytes 62984 | tf_op jit(solution)/shard_map/ppermute | solution.py:14
  20.3 5.8 %collective-permute-start.1 = (f32[41,128]{1,0:T(8,128)S(1)}, f32[41,128]{1,0:T(8,128)S(1)}, u32[]{:S(2)}, u32[]{:S(2)}) collective-permute-start(f32[41,128]{1,0:T(8,128)S(1)} %bitcast.100), channel_id=1, source_target_pairs={{0,16},{16,32},{32,48},{48,64},{64,80},{80,96},{96,112},{112,128},... | collective-permute-start | bytes 62984 | tf_op jit(solution)/shard_map/ppermute | solution.py:14
  23.4 4.7 %collective-permute-start.2 = (f32[41,128]{1,0:T(8,128)S(1)}, f32[41,128]{1,0:T(8,128)S(1)}, u32[]{:S(2)}, u32[]{:S(2)}) collective-permute-start(f32[41,128]{1,0:T(8,128)S(1)} %bitcast.101), channel_id=1, source_target_pairs={{16,0},{32,16},{48,32},{64,48},{80,64},{96,80},{112,96},{128,112},... | collective-permute-start | bytes 62984 | tf_op jit(solution)/shard_map/ppermute | solution.py:14
  24.7 6.5 %collective-permute-start.3 = (f32[41,128]{1,0:T(8,128)S(1)}, f32[41,128]{1,0:T(8,128)S(1)}, u32[]{:S(2)}, u32[]{:S(2)}) collective-permute-start(f32[41,128]{1,0:T(8,128)S(1)} %bitcast.102), channel_id=1, source_target_pairs={{32,0},{48,16},{64,32},{80,48},{96,64},{112,80},{128,96},{144,112}... | collective-permute-start | bytes 62984 | tf_op jit(solution)/shard_map/ppermute | solution.py:14
  31.7 2.1 slice-start
  34.7 2.3 copy-start.6
  34.7 2.3 copy-start.11
  35.0 5.3 %copy-start.8 = (pred[512]{0:T(512)(128)(4,1)S(1)}, pred[512]{0:T(512)(128)(4,1)}, u32[]{:S(2)}) copy-start(pred[512]{0:T(512)(128)(4,1)} %copy-done.7) | copy-start | bytes 1540
  42.3 87.6 %copy-start.2 = (s32[1,4,128]{2,1,0:T(4,128)S(1)}, s32[1,4,128]{2,1,0:T(4,128)}, u32[]{:S(2)}) copy-start(s32[1,4,128]{2,1,0:T(4,128)} %param.17) | copy-start | bytes 6148
  308.0 8.2 %copy-start.4 = (f32[4096]{0:T(1024)S(1)}, f32[4096]{0:T(1024)}, u32[]{:S(2)}) copy-start(f32[4096]{0:T(1024)} %copy-done.3) | copy-start | bytes 49156
Sparse Core Ops, SparseCore 0:
  32.7 87.9 all-gather.2
where the time goes:
time: 328 us; the launch traced here: 324 us
  matrix products  85.4 us (26%)
  waiting for transfers between devices  83.6 us (25%)
  other arithmetic  69.2 us (21%)
  local copies, waits for them, and re-layouts  59.3 us (18%)
  between operations  14.5 us (4%)
  starting transfers between devices  10.1 us (3%)
    dot_general x12, matrix products, one_term(): jnp.dot(mixing_rows[kl_index], portion, precision=HIGHEST, preferred_elem...  85.4 us
    all_gather x1, waiting for transfers between devices, per_device(): portion = lax.all_gather(extended, 'mode', axis=0, tiled=True)  78.4 us
    add x24, other arithmetic, one_term(): return (partial_value[0] + grid_part, partial_value[1] + face_part)  22.1 us
    gather x24, local copies, waits for them, and re-layouts, operator_terms(): own_values = jnp.take(inside, own_flat, axis=1)  13.8 us
    unnamed x34, local copies, waits for them, and re-layouts  11.7 us
    mul x26, other arithmetic, grid_terms(): 0.5 * (conduct[..., 1:, :] + conduct[..., :-1, :])  10.8 us
    mul x13, other arithmetic, grid_terms(): 0.5 * (conduct[..., :, 1:] + conduct[..., :, :-1])  10.2 us
    ppermute x4, starting transfers between devices, shifted(): lax.ppermute(value, axis, [(source, source + steps) for source in range(f...  10.1 us
  transfers between devices with their start and end apart: 5, of which 3 were waited for; matrix products, arithmetic and copies ran while one was open for 3% of the time, Pallas kernels for 0%

commit v1 on v0

--- a/solution.py
+++ b/solution.py
@@ -6,6 +6,12 @@
 GZ = 128
 SLOT_OFFSETS = (-2, -1, 1, 2)
 HIGHEST = lax.Precision.HIGHEST
+
+
+def islands_wait(vals):
+    heard = jnp.stack(lax.axis_size("mode") * [vals])
+    right_arr = lax.all_to_all(heard, "mode", 0, 0)
+    return jnp.concatenate(right_arr, axis=0)
 
 
 def shifted(value, axis, steps):
@@ -93,7 +99,7 @@
         jnp.zeros((modes_here, cells_here), jnp.float32),
         jnp.zeros((modes_here, 4 * face_limit), jnp.float32),
     )
-    portion = lax.all_gather(extended, "mode", axis=0, tiled=True)
+    portion = islands_wait(extended)
 
     def one_term(kl_index, partial_value):
         mixed_part = jnp.dot(

time: 328 us -> 348 us (1.061)
  waiting for transfers between devices: 83.6 us -> 103 us
  between operations: 14.5 us -> 1.12 us
  starting transfers between devices: 10.1 us -> 19.5 us
  local copies, waits for them, and re-layouts: 59.3 us -> 64.1 us
    all_to_all x0 -> x1, waiting for transfers between devices: none -> 97.6 us  [islands_wait(): right_arr = lax.all_to_all(heard, 'mode', 0, 0)]
    all_gather x1 -> x0, waiting for transfers between devices: 78.4 us -> none  [per_device(): portion = lax.all_gather(extended, 'mode', axis=0, tiled=True)]
    all_to_all x0 -> x1, starting transfers between devices: none -> 9.44 us  [islands_wait(): right_arr = lax.all_to_all(heard, 'mode', 0, 0)]
    unnamed x34 -> x33, local copies, waits for them, and re-layouts: 11.7 us -> 2.45 us
    reshape x0 -> x1, local copies, waits for them, and re-layouts: none -> 9.25 us  [islands_wait(): return jnp.concatenate(right_arr, axis=0)]
    another operation x1 -> x2, local copies, waits for them, and re-layouts: 0.21 us -> 5.01 us  [the longest x1 4.8 us: islands_wait(): heard = jnp.stack(lax.axis_size('mode') * [vals])]
where the time goes in v1:
time: 348 us; the launch traced here: 343 us
  waiting for transfers between devices  103 us (30%)
  matrix products  85.4 us (25%)
  other arithmetic  68.4 us (20%)
  local copies, waits for them, and re-layouts  64.1 us (18%)
  starting transfers between devices  19.5 us (6%)
    all_to_all x1, waiting for transfers between devices, islands_wait(): right_arr = lax.all_to_all(heard, 'mode', 0, 0)  97.6 us
    dot_general x12, matrix products, one_term(): jnp.dot(mixing_rows[kl_index], portion, precision=HIGHEST, preferred_elem...  85.4 us
    add x24, other arithmetic, one_term(): return (partial_value[0] + grid_part, partial_value[1] + face_part)  22.1 us
    gather x24, local copies, waits for them, and re-layouts, operator_terms(): own_values = jnp.take(inside, own_flat, axis=1)  13.8 us
    mul x26, other arithmetic, grid_terms(): 0.5 * (conduct[..., 1:, :] + conduct[..., :-1, :])  10.8 us
    mul x13, other arithmetic, grid_terms(): 0.5 * (conduct[..., :, 1:] + conduct[..., :, :-1])  10.2 us
    ppermute x4, starting transfers between devices, shifted(): lax.ppermute(value, axis, [(source, source + steps) for source in range(f...  10.1 us
    all_to_all x1, starting transfers between devices, islands_wait(): right_arr = lax.all_to_all(heard, 'mode', 0, 0)  9.44 us
  transfers between devices with their start and end apart: 5, of which 3 were waited for; matrix products, arithmetic and copies ran while one was open for 3% of the time, Pallas kernels for 0%

profile of v1, /device:TPU:1, one launch (start us, length us, event | category | flops | bytes accessed | tf_op | source)
XLA Modules:
  0.0 343.1 jit_solution(16387069374871193259)
XLA Ops:
  9.3 4.4 %collective-permute-start = (f32[41,128]{1,0:T(8,128)S(1)}, f32[41,128]{1,0:T(8,128)S(1)}, u32[]{:S(2)}, u32[]{:S(2)}) collective-permute-start(f32[41,128]{1,0:T(8,128)S(1)} %bitcast.97), channel_id=1, source_target_pairs={{0,32},{16,48},{32,64},{48,80},{64,96},{80,112},{96,128},{112,144}... | collective-permute-start | bytes 62984 | tf_op jit(solution)/shard_map/ppermute | solution.py:20
  13.7 3.1 collective-permute-start.1
  21.6 3.1 collective-permute-done.3
  25.2 4.8 %stack.17 = f32[16,28,4608]{2,1,0:T(8,128)} broadcast(f32[28,4608]{1,0:T(8,128)S(1)} %pad_maximum_fusion), dimensions={1,2} | broadcast | bytes 8773632 | tf_op jit(solution)/shard_map/stack | solution.py:12
  30.0 9.4 %all-to-all-start = ((f32[16,28,4608]{2,1,0:T(8,128)}), f32[16,28,4608]{2,1,0:T(8,128)}, u32[]{:S(2)}, u32[]{:S(2)}) async-start(f32[16,28,4608]{2,1,0:T(8,128)} %stack.17), calls=%async_computation | async-start | bytes 18874368 | tf_op jit(solution)/shard_map/all_to_all | solution.py:13
  43.9 3.0 fusion.12
  49.1 97.6 %all-to-all-done = f32[16,28,4608]{2,1,0:T(8,128)} async-done(((f32[16,28,4608]{2,1,0:T(8,128)}), f32[16,28,4608]{2,1,0:T(8,128)}, u32[]{:S(2)}, u32[]{:S(2)}) %all-to-all-start) | async-done | bytes 8257568 | tf_op jit(solution)/shard_map/all_to_all | solution.py:13
  146.7 9.3 %reshape.135 = f32[448,4608]{1,0:T(8,128)} reshape(f32[16,28,4608]{2,1,0:T(8,128)} %all-to-all-done) | data formatting | bytes 16515072 | tf_op jit(solution)/shard_map/reshape | solution.py:14
  155.9 171.5 %while.18 = (s32[]{:T(128)}, f32[28,4096]{1,0:T(8,128)}, f32[28,512]{1,0:T(8,128)S(1)}, f32[13,4096]{1,0:T(8,128)S(1)}, f32[31,128]{1,0:T(8,128)}, /*index=5*/f3...) while((s32[]{:T(128)}, f32[28,4096]{1,0:T(8,128)}, ...), condition=%wide.region_2.4_spmd.clone, body=%wide.region_1.3_spmd.clone.sunk | while | flops 694757632 | bytes 20811360 | solution.py:118
  156.8 7.1 %fusion.31 = f32[28,4608]{1,0:T(8,128)S(1)} fusion(f32[448,4608]{1,0:T(8,128)} %get-tuple-element.445, f32[12,28,448]{2,1,0:T(8,128)} %get-tuple-element.444, s32[]{:T(128)} %get-tuple-element.424), kind=kOutput, calls=%fused_computation.13.clone.1 | convolution fusion | flops 693633024 | bytes 8839680 | tf_op jit(solution)/shard_map/while/body/eval_jaxpr/dot_general | solution.py:105
  170.1 7.1 %fusion.31 = f32[28,4608]{1,0:T(8,128)S(1)} fusion(f32[448,4608]{1,0:T(8,128)} %get-tuple-element.445, f32[12,28,448]{2,1,0:T(8,128)} %get-tuple-element.444, s32[]{:T(128)} %get-tuple-element.424), kind=kOutput, calls=%fused_computation.13.clone.1 | convolution fusion | flops 693633024 | bytes 8839680 | tf_op jit(solution)/shard_map/while/body/eval_jaxpr/dot_general | solution.py:105
  184.5 7.1 %fusion.31 = f32[28,4608]{1,0:T(8,128)S(1)} fusion(f32[448,4608]{1,0:T(8,128)} %get-tuple-element.445, f32[12,28,448]{2,1,0:T(8,128)} %get-tuple-element.444, s32[]{:T(128)} %get-tuple-element.424), kind=kOutput, calls=%fused_computation.13.clone.1 | convolution fusion | flops 693633024 | bytes 8839680 | tf_op jit(solution)/shard_map/while/body/eval_jaxpr/dot_general | solution.py:105
  198.9 7.1 %fusion.31 = f32[28,4608]{1,0:T(8,128)S(1)} fusion(f32[448,4608]{1,0:T(8,128)} %get-tuple-element.445, f32[12,28,448]{2,1,0:T(8,128)} %get-tuple-element.444, s32[]{:T(128)} %get-tuple-element.424), kind=kOutput, calls=%fused_computation.13.clone.1 | convolution fusion | flops 693633024 | bytes 8839680 | tf_op jit(solution)/shard_map/while/body/eval_jaxpr/dot_general | solution.py:105
  213.3 7.1 %fusion.31 = f32[28,4608]{1,0:T(8,128)S(1)} fusion(f32[448,4608]{1,0:T(8,128)} %get-tuple-element.445, f32[12,28,448]{2,1,0:T(8,128)} %get-tuple-element.444, s32[]{:T(128)} %get-tuple-element.424), kind=kOutput, calls=%fused_computation.13.clone.1 | convolution fusion | flops 693633024 | bytes 8839680 | tf_op jit(solution)/shard_map/while/body/eval_jaxpr/dot_general | solution.py:105
  227.7 7.1 %fusion.31 = f32[28,4608]{1,0:T(8,128)S(1)} fusion(f32[448,4608]{1,0:T(8,128)} %get-tuple-element.445, f32[12,28,448]{2,1,0:T(8,128)} %get-tuple-element.444, s32[]{:T(128)} %get-tuple-element.424), kind=kOutput, calls=%fused_computation.13.clone.1 | convolution fusion | flops 693633024 | bytes 8839680 | tf_op jit(solution)/shard_map/while/body/eval_jaxpr/dot_general | solution.py:105
  242.1 7.1 %fusion.31 = f32[28,4608]{1,0:T(8,128)S(1)} fusion(f32[448,4608]{1,0:T(8,128)} %get-tuple-element.445, f32[12,28,448]{2,1,0:T(8,128)} %get-tuple-element.444, s32[]{:T(128)} %get-tuple-element.424), kind=kOutput, calls=%fused_computation.13.clone.1 | convolution fusion | flops 693633024 | bytes 8839680 | tf_op jit(solution)/shard_map/while/body/eval_jaxpr/dot_general | solution.py:105
  256.4 7.1 %fusion.31 = f32[28,4608]{1,0:T(8,128)S(1)} fusion(f32[448,4608]{1,0:T(8,128)} %get-tuple-element.445, f32[12,28,448]{2,1,0:T(8,128)} %get-tuple-element.444, s32[]{:T(128)} %get-tuple-element.424), kind=kOutput, calls=%fused_computation.13.clone.1 | convolution fusion | flops 693633024 | bytes 8839680 | tf_op jit(solution)/shard_map/while/body/eval_jaxpr/dot_general | solution.py:105
  270.8 7.1 %fusion.31 = f32[28,4608]{1,0:T(8,128)S(1)} fusion(f32[448,4608]{1,0:T(8,128)} %get-tuple-element.445, f32[12,28,448]{2,1,0:T(8,128)} %get-tuple-element.444, s32[]{:T(128)} %get-tuple-element.424), kind=kOutput, calls=%fused_computation.13.clone.1 | convolution fusion | flops 693633024 | bytes 8839680 | tf_op jit(solution)/shard_map/while/body/eval_jaxpr/dot_general | solution.py:105
  285.2 7.1 %fusion.31 = f32[28,4608]{1,0:T(8,128)S(1)} fusion(f32[448,4608]{1,0:T(8,128)} %get-tuple-element.445, f32[12,28,448]{2,1,0:T(8,128)} %get-tuple-element.444, s32[]{:T(128)} %get-tuple-element.424), kind=kOutput, calls=%fused_computation.13.clone.1 | convolution fusion | flops 693633024 | bytes 8839680 | tf_op jit(solution)/shard_map/while/body/eval_jaxpr/dot_general | solution.py:105
  299.6 7.1 %fusion.31 = f32[28,4608]{1,0:T(8,128)S(1)} fusion(f32[448,4608]{1,0:T(8,128)} %get-tuple-element.445, f32[12,28,448]{2,1,0:T(8,128)} %get-tuple-element.444, s32[]{:T(128)} %get-tuple-element.424), kind=kOutput, calls=%fused_computation.13.clone.1 | convolution fusion | flops 693633024 | bytes 8839680 | tf_op jit(solution)/shard_map/while/body/eval_jaxpr/dot_general | solution.py:105
  314.0 7.1 %fusion.31 = f32[28,4608]{1,0:T(8,128)S(1)} fusion(f32[448,4608]{1,0:T(8,128)} %get-tuple-element.445, f32[12,28,448]{2,1,0:T(8,128)} %get-tuple-element.444, s32[]{:T(128)} %get-tuple-element.424), kind=kOutput, calls=%fused_computation.13.clone.1 | convolution fusion | flops 693633024 | bytes 8839680 | tf_op jit(solution)/shard_map/while/body/eval_jaxpr/dot_general | solution.py:105
  328.6 3.0 copy.83
  331.6 2.4 bitcast_add_fusion
  334.0 7.6 %scatter_fusion = f32[28,4096]{0,1:T(8,128)S(1)} fusion(f32[28,4096]{0,1:T(8,128)S(1)} %bitcast_add_fusion, s32[1024]{0:T(1024)S(1)} %bitcast.102, f32[1024,28]{1,0:T(8,128)S(1)} %copy.85), kind=kCustom, calls=%fused_computation.3 | custom fusion | flops 28672 | bytes 348160 | tf_op jit(solution)/shard_map/add | solution.py:119
  (341 shorter events, 107.1 us)
Async XLA Ops:
  1.4 6.7 %copy-start.7 = (pred[512]{0:T(512)(128)(4,1)}, pred[512]{0:T(512)(128)(4,1)S(1)}, u32[]{:S(2)}) copy-start(pred[512]{0:T(512)(128)(4,1)S(1)} %compare_and_fusion.1) | copy-start | bytes 1540
  2.0 0.6 copy-start.3
  3.7 2.6 copy-start.1
  3.7 2.6 copy-start
  6.4 1.9 copy-start.5
  9.3 10.1 %collective-permute-start = (f32[41,128]{1,0:T(8,128)S(1)}, f32[41,128]{1,0:T(8,128)S(1)}, u32[]{:S(2)}, u32[]{:S(2)}) collective-permute-start(f32[41,128]{1,0:T(8,128)S(1)} %bitcast.97), channel_id=1, source_target_pairs={{0,32},{16,48},{32,64},{48,80},{64,96},{80,112},{96,128},{112,144}... | collective-permute-start | bytes 62984 | tf_op jit(solution)/shard_map/ppermute | solution.py:20
  13.7 5.8 %collective-permute-start.1 = (f32[41,128]{1,0:T(8,128)S(1)}, f32[41,128]{1,0:T(8,128)S(1)}, u32[]{:S(2)}, u32[]{:S(2)}) collective-permute-start(f32[41,128]{1,0:T(8,128)S(1)} %bitcast.98), channel_id=1, source_target_pairs={{0,16},{16,32},{32,48},{48,64},{64,80},{80,96},{96,112},{112,128},... | collective-permute-start | bytes 62984 | tf_op jit(solution)/shard_map/ppermute | solution.py:20
  16.9 4.7 %collective-permute-start.2 = (f32[41,128]{1,0:T(8,128)S(1)}, f32[41,128]{1,0:T(8,128)S(1)}, u32[]{:S(2)}, u32[]{:S(2)}) collective-permute-start(f32[41,128]{1,0:T(8,128)S(1)} %bitcast.99), channel_id=1, source_target_pairs={{16,0},{32,16},{48,32},{64,48},{80,64},{96,80},{112,96},{128,112},... | collective-permute-start | bytes 62984 | tf_op jit(solution)/shard_map/ppermute | solution.py:20
  18.2 6.5 %collective-permute-start.3 = (f32[41,128]{1,0:T(8,128)S(1)}, f32[41,128]{1,0:T(8,128)S(1)}, u32[]{:S(2)}, u32[]{:S(2)}) collective-permute-start(f32[41,128]{1,0:T(8,128)S(1)} %bitcast.100), channel_id=1, source_target_pairs={{32,0},{48,16},{64,32},{80,48},{96,64},{112,80},{128,96},{144,112}... | collective-permute-start | bytes 62984 | tf_op jit(solution)/shard_map/ppermute | solution.py:20
  30.0 9.5 %copy-start.9 = (s32[12,2,28]{2,1,0:T(2,128)S(1)}, s32[12,2,28]{2,1,0:T(2,128)}, u32[]{:S(2)}) copy-start(s32[12,2,28]{2,1,0:T(2,128)} %param.13) | copy-start | bytes 8068
  30.0 9.7 %copy-start.10 = (f32[12,2,28]{2,1,0:T(2,128)S(1)}, f32[12,2,28]{2,1,0:T(2,128)}, u32[]{:S(2)}) copy-start(f32[12,2,28]{2,1,0:T(2,128)} %param.14) | copy-start | bytes 8068
  30.0 116.7 %all-to-all-start = ((f32[16,28,4608]{2,1,0:T(8,128)}), f32[16,28,4608]{2,1,0:T(8,128)}, u32[]{:S(2)}, u32[]{:S(2)}) async-start(f32[16,28,4608]{2,1,0:T(8,128)} %stack.17), calls=%async_computation | async-start | bytes 18874368 | tf_op jit(solution)/shard_map/all_to_all | solution.py:13
  39.4 1.2 slice-start
  41.6 2.2 copy-start.6
  41.6 2.2 copy-start.11
  41.8 5.3 %copy-start.8 = (pred[512]{0:T(512)(128)(4,1)S(1)}, pred[512]{0:T(512)(128)(4,1)}, u32[]{:S(2)}) copy-start(pred[512]{0:T(512)(128)(4,1)} %copy-done.7) | copy-start | bytes 1540
  49.1 106.8 %copy-start.2 = (s32[1,4,128]{2,1,0:T(4,128)S(1)}, s32[1,4,128]{2,1,0:T(4,128)}, u32[]{:S(2)}) copy-start(s32[1,4,128]{2,1,0:T(4,128)} %param.17) | copy-start | bytes 6148
  334.0 8.2 %copy-start.4 = (f32[4096]{0:T(1024)S(1)}, f32[4096]{0:T(1024)}, u32[]{:S(2)}) copy-start(f32[4096]{0:T(1024)} %copy-done.3) | copy-start | bytes 49156
